TPU v7x, 256 devices: a whole 4x4x8 slice. The times are simulated.
256 devices in a mesh: tile: 32 (over z, x_hi, core), group: 8 (over y, x_lo).
Axes of the slice: x: 4 (x_hi: 2, x_lo: 2; x = x_hi * 2 + x_lo), y: 4, z: 8, core: 2. Of those that a mesh axis runs over, the one named last changes fastest.
Arguments:
- object_field: float32 [2, 320, 4096], P(None, 'group', 'tile'), may hold values from -6 to 6
- probe_field: float32 [2, 256, 256], replicated, may hold values from -6 to 6
- amplitudes: float32 [256, 256, 256], P(('tile', 'group')), may hold values from 0 to 4
- row_start: int32 [256], P(('tile', 'group')), may hold values from 0 to 64
- column_start: int32 [256], P(('tile', 'group')), may hold values from 0 to 128
- live_slots: int32 [256], P(('tile', 'group')), may hold values 0 or 1
Outputs:
- new_object: float32 [2, 320, 4096], P(None, 'group', 'tile')
- new_probe: float32 [2, 256, 256], replicated
All inputs are finite; a program needn't handle non-finite values. No bound on the sum of `live_slots` on one device may be relied on, other than what follows from the above.
Results may differ from a plain program's by a relative error of at most 0.0001.
Values sent between devices are 32-bit elements; how exact they have to be, the bound alone decides.
No kernel may reach another device: no remote copies, remote signals or barrier semaphores. Data moves between devices by JAX's collectives and lax.ppermute only.
A program may use at most 64 MiB of HBM per device.

v0:
```python
import math
import jax
import jax.numpy as jnp
from jax import lax
from jax.sharding import PartitionSpec as P

WIN = 256
HALO = 128


def padded_2(value, sides, width):
    for axis, dim in sides:
        count, length = (lax.axis_size(axis), value.shape[dim])
        up = [(i, (i + 1) % count) for i in range(count - 1)]
        down = [(j, i) for i, j in up]
        last = lax.slice_in_dim(value, length - width, length, axis=dim)
        initial = lax.slice_in_dim(value, 0, width, axis=dim)
        before = lax.ppermute(last, axis, up)
        after = lax.ppermute(initial, axis, down)
        value = jnp.concatenate([before, value, after], axis=dim)
    return value


def dft_tables(length):
    counter = jnp.arange(length, dtype=jnp.int32)
    product = counter[:, None] * counter[None, :] % length
    angles = 2.0 * math.pi / length * product.astype(jnp.float32)
    factor = 1.0 / math.sqrt(length)
    return (jnp.cos(angles) * factor, jnp.sin(angles) * factor)


def apply_left(matrix, values):
    return jnp.einsum("jk,pkl->pjl", matrix, values, precision=lax.Precision.HIGHEST)


def apply_right(values, matrix):
    return jnp.einsum("pjk,kl->pjl", values, matrix, precision=lax.Precision.HIGHEST)


def transform(real_part, imag_part, cos_table, sin_table, sign):
    left_real = apply_left(cos_table, real_part) - sign * apply_left(sin_table, imag_part)
    left_imag = apply_left(cos_table, imag_part) + sign * apply_left(sin_table, real_part)
    right_real = apply_right(left_real, cos_table) - sign * apply_right(left_imag, sin_table)
    right_imag = apply_right(left_imag, cos_table) + sign * apply_right(left_real, sin_table)
    return (right_real, right_imag)


def window_terms(windows, probe_field, amplitudes, live_slots, cos_table, sin_table):
    sample_real = windows[:, 0]
    sample_imag = windows[:, 1]
    probe_real = probe_field[0]
    probe_imag = probe_field[1]
    exit_real = probe_real * sample_real - probe_imag * sample_imag
    exit_imag = probe_real * sample_imag + probe_imag * sample_real
    far_real, far_imag = transform(exit_real, exit_imag, cos_table, sin_table, -1.0)
    modulus = jnp.maximum(jnp.sqrt(far_real * far_real + far_imag * far_imag), 0.25)
    factor = 1.0 - amplitudes / modulus
    miss_real, miss_imag = transform(
        far_real * factor, far_imag * factor, cos_table, sin_table, 1.0
    )
    weight = live_slots.astype(jnp.float32)[:, None, None]
    miss_real = miss_real * weight
    miss_imag = miss_imag * weight
    grad_real = probe_real * miss_real + probe_imag * miss_imag
    grad_imag = probe_real * miss_imag - probe_imag * miss_real
    probe_light = weight * (probe_real * probe_real + probe_imag * probe_imag)
    terms = jnp.stack([grad_real, grad_imag, probe_light], axis=1)
    probe_grad = jnp.stack(
        [
            jnp.sum(sample_real * miss_real + sample_imag * miss_imag, axis=0),
            jnp.sum(sample_real * miss_imag - sample_imag * miss_real, axis=0),
        ],
        axis=0,
    )
    window_light = jnp.sum(weight * (sample_real * sample_real + sample_imag * sample_imag), axis=0)
    return (terms, probe_grad, window_light)


def add_windows(accum, terms, top_rows, left_edges):
    zero_index = jnp.zeros((), jnp.int32)
    channels = terms.shape[1]

    def place(slot, current):
        corner = (zero_index, top_rows[slot], left_edges[slot])
        piece = lax.dynamic_slice(current, corner, (channels, WIN, WIN))
        return lax.dynamic_update_slice(current, piece + terms[slot], corner)

    return lax.fori_loop(0, terms.shape[0], place, accum)


def cut_windows(padded, top_rows, left_edges):
    zero_index = jnp.zeros((), jnp.int32)

    def single(top_row, left_edge):
        return lax.dynamic_slice(padded, (zero_index, top_row, left_edge), (2, WIN, WIN))

    return jax.vmap(single)(top_rows, left_edges)


def edge_strips(accum):
    return jnp.concatenate([accum[:, :, :HALO], accum[:, :, accum.shape[2] - HALO :]], axis=2)


def add_edges(inner, arrived):
    width = inner.shape[2]
    inner = inner.at[:, :, :HALO].add(arrived[:, :, :HALO])
    return inner.at[:, :, width - HALO :].add(arrived[:, :, arrived.shape[2] - HALO :])


def apply_updates(object_field, probe_field, share, probe_grad, window_light):
    light_max = jnp.max(probe_field[0] * probe_field[0] + probe_field[1] * probe_field[1]) + 1e-06
    new_object = object_field - share[0:2] / (share[2:3] + 0.25 * light_max)
    new_probe = (
        probe_field - probe_grad / (window_light + 0.25 * jnp.mean(window_light) + 1e-05)[None]
    )
    return (new_object, new_probe)


def local(object_field, probe_field, amplitudes, row_start, column_start, live_slots):
    cos_table, sin_table = dft_tables(WIN)
    full_rows = lax.all_gather(object_field, "group", axis=1, tiled=True)
    padded = padded_2(full_rows, (("tile", 2),), HALO)
    windows = cut_windows(padded, row_start, column_start)
    terms, probe_grad, window_light = window_terms(
        windows, probe_field, amplitudes, live_slots, cos_table, sin_table
    )
    accum = jnp.zeros((terms.shape[1], padded.shape[1], padded.shape[2]), jnp.float32)
    accum = add_windows(accum, terms, row_start, column_start)
    arrived = padded_2(edge_strips(accum), (("tile", 2),), HALO)
    summed = add_edges(accum[:, :, HALO : accum.shape[2] - HALO], arrived)
    share = lax.psum_scatter(summed, "group", scatter_dimension=1, tiled=True)
    probe_grad, window_light = lax.psum((probe_grad, window_light), ("tile", "group"))
    object_field, probe_field = apply_updates(
        object_field, probe_field, share, probe_grad, window_light
    )
    return (object_field, probe_field)


def solution(mesh):
    return jax.shard_map(
        local,
        mesh=mesh,
        in_specs=(
            P(None, "group", "tile"),
            P(),
            P(("tile", "group"), None, None),
            P(("tile", "group")),
            P(("tile", "group")),
            P(("tile", "group")),
        ),
        out_specs=(P(None, "group", "tile"), P()),
        check_vma=False,
    )
```

profile of v0, /device:TPU:2, one launch (start us, length us, event | category | flops | bytes accessed | tf_op | source)
XLA Modules:
  0.0 370.7 jit_solution(3378128131235949026)
XLA Ops:
  8.1 29.8 %all_gather.3 = f32[2,320,128]{2,1,0:T(8,128)S(1)} all-gather(f32[2,40,128]{2,1,0:T(8,128)} %param.14), channel_id=1, replica_groups=mesh['tile'=32,'group'=8] {'group'}, dimensions={1}, use_global_device_ids=true | all-gather | bytes 368640 | tf_op jit(solution)/shard_map/all_gather | solution.py:121
  39.2 3.1 collective-permute-start
  44.7 1.5 fusion.38
  46.2 1.5 fusion.34
  47.7 1.5 fusion.9
  49.2 1.5 fusion.7
  50.7 1.5 fusion.47
  52.2 1.5 fusion.48
  53.6 1.5 fusion.4
  55.1 1.7 bitcast_multiply_fusion.11
  58.4 1.5 fusion.27
  59.8 1.5 fusion.3
  61.3 1.5 fusion.2
  62.8 1.5 fusion.45
  64.3 1.5 fusion.46
  65.8 1.5 fusion
  67.3 1.7 fusion.1
  69.9 10.9 %dynamic_update_slice.4 = f32[3,320,384]{2,1,0:T(8,128)S(1)} dynamic-update-slice(f32[3,320,384]{2,1,0:T(8,128)S(1)} %broadcast_in_dim.6, f32[3,256,256]{2,1,0:T(8,128)S(1)} %maximum_bitcast_fusion, s32[]{:T(128)} %constant.112.clone.1, s32[]{:T(128)S(6)} %select_n.60, s32[]{:T(128)S(6)} %select_n.61) | dynamic-update-slice | bytes 1572868 | tf_op jit(solution)/shard_map/while/body/eval_jaxpr/dynamic_update_slice | solution.py:86
  81.6 6.6 %collective-permute-start.2 = (f32[3,320,128]{2,1,0:T(8,128)}, f32[3,320,128]{2,1,0:T(8,128)S(1)}, u32[]{:S(2)}, u32[]{:S(2)}) collective-permute-start(f32[3,320,128]{2,1,0:T(8,128)} %get-tuple-element.73), channel_id=1, source_target_pairs={{0,8},{8,16},{16,24},{24,32},{32,40},{40,48},{48,56},{56,64},{64,7... | collective-permute-start | bytes 1474568 | tf_op jit(solution)/shard_map/ppermute | solution.py:18
  91.3 4.5 %collective-permute-done.3 = f32[3,320,128]{2,1,0:T(8,128)} collective-permute-done((f32[3,320,128]{2,1,0:T(8,128)S(1)}, f32[3,320,128]{2,1,0:T(8,128)}, u32[]{:S(2)}, u32[]{:S(2)}) %collective-permute-start.3) | collective-permute-done | bytes 491552 | tf_op jit(solution)/shard_map/ppermute | solution.py:19
  95.7 1.9 fusion.13
  98.3 257.6 %all-reduce.3.cloned.1.call-done = (f32[2,256,256]{2,1,0:T(8,128)}, f32[256,256]{1,0:T(8,128)}) async-done(((f32[2,256,256]{2,1,0:T(8,128)}, f32[256,256]{1,0:T(8,128)}), (f32[2,256,256]{2,1,0:T(8,128)}, f32[256,256]{1,0:T(8,128)})) %all-reduce.3.cloned.1.call-update) | async-done | bytes 786448 | tf_op jit(solution)/shard_map/psum | solution.py:132
  355.9 1.6 reduce_sum.8
  359.2 1.9 divide_subtract_fusion
  (36 shorter events, 11.2 us)
Async XLA Ops:
  8.0 36.6 %copy-start = (f32[2,256,256]{2,1,0:T(8,128)S(1)}, f32[2,256,256]{2,1,0:T(8,128)}, u32[]{:S(2)}) copy-start(f32[2,256,256]{2,1,0:T(8,128)} %param.15) | copy-start | bytes 1572868
  8.0 347.9 %all-reduce.3.cloned.1.call-start = ((), (), s32[]{:S(2)}) async-start(), calls=%async_computation.2 | async-start | bytes 1572864 | tf_op jit(solution)/shard_map/psum | solution.py:132
  37.9 6.3 %collective-permute-start.1 = (f32[2,320,128]{2,1,0:T(8,128)S(1)}, f32[2,320,128]{2,1,0:T(8,128)S(1)}, u32[]{:S(2)}, u32[]{:S(2)}) collective-permute-start(f32[2,320,128]{2,1,0:T(8,128)S(1)} %all_gather.3), channel_id=1, source_target_pairs={{8,0},{16,8},{24,16},{32,24},{40,32},{48,40},{56,48},{64,56},{72,6... | collective-permute-start | bytes 983048 | tf_op jit(solution)/shard_map/ppermute | solution.py:19
  39.2 5.0 %collective-permute-start = (f32[2,320,128]{2,1,0:T(8,128)S(1)}, f32[2,320,128]{2,1,0:T(8,128)S(1)}, u32[]{:S(2)}, u32[]{:S(2)}) collective-permute-start(f32[2,320,128]{2,1,0:T(8,128)S(1)} %all_gather.3), channel_id=1, source_target_pairs={{0,8},{8,16},{16,24},{24,32},{32,40},{40,48},{48,56},{56,64},{64,7... | collective-permute-start | bytes 983048 | tf_op jit(solution)/shard_map/ppermute | solution.py:18
  52.1 3.0 copy-start.6
  67.3 2.4 copy-start.1
  69.0 0.8 copy-start.3
  80.8 8.8 %copy-start.2 = (f32[256,256]{1,0:T(8,128)S(1)}, f32[256,256]{1,0:T(8,128)}, u32[]{:S(2)}) copy-start(f32[256,256]{1,0:T(8,128)} %copy-done.1) | copy-start | bytes 786436
  80.8 8.8 %copy-start.4 = (f32[256,256]{1,0:T(8,128)S(1)}, f32[256,256]{1,0:T(8,128)}, u32[]{:S(2)}) copy-start(f32[256,256]{1,0:T(8,128)} %copy-done.3) | copy-start | bytes 786436
  81.6 9.6 %collective-permute-start.2 = (f32[3,320,128]{2,1,0:T(8,128)}, f32[3,320,128]{2,1,0:T(8,128)S(1)}, u32[]{:S(2)}, u32[]{:S(2)}) collective-permute-start(f32[3,320,128]{2,1,0:T(8,128)} %get-tuple-element.73), channel_id=1, source_target_pairs={{0,8},{8,16},{16,24},{24,32},{32,40},{40,48},{48,56},{56,64},{64,7... | collective-permute-start | bytes 1474568 | tf_op jit(solution)/shard_map/ppermute | solution.py:18
  88.2 7.5 %collective-permute-start.3 = (f32[3,320,128]{2,1,0:T(8,128)S(1)}, f32[3,320,128]{2,1,0:T(8,128)}, u32[]{:S(2)}, u32[]{:S(2)}) collective-permute-start(f32[3,320,128]{2,1,0:T(8,128)S(1)} %get-tuple-element.74), channel_id=1, source_target_pairs={{8,0},{16,8},{24,16},{32,24},{40,32},{48,40},{56,48},{64,56},{72,6... | collective-permute-start | bytes 1474568 | tf_op jit(solution)/shard_map/ppermute | solution.py:19
  91.2 269.9 %reduce-scatter.2.cloned.1.call-start = ((), (), s32[]{:S(2)}) async-start(), calls=%async_computation.1 | async-start | bytes 552960 | tf_op jit(solution)/shard_map/reduce_scatter | solution.py:131
  97.6 264.2 %copy-start.5 = (f32[2,40,128]{2,1,0:T(8,128)S(1)}, f32[2,40,128]{2,1,0:T(8,128)}, u32[]{:S(2)}) copy-start(f32[2,40,128]{2,1,0:T(8,128)} %param.14) | copy-start | bytes 122884
Sparse Core Ops, SparseCore 0:
  91.3 264.5 all-reduce.2
Sparse Core Ops, SparseCore 1:
  97.8 51.0 reduce-scatter.1
where the time goes:
time: 371 us
  waiting for transfers between devices  262 us (71%)
  blocking collectives  29.8 us (8%)
  matrix products  24.1 us (6%)
  between operations  19 us (5%)
  starting transfers between devices  12.3 us (3%)
  local copies, waits for them, and re-layouts  11.9 us (3%)
  other arithmetic  11.4 us (3%)
    psum x1, waiting for transfers between devices, local(): lax.psum((probe_grad, window_light), ('tile', 'group'))  258 us
    all_gather x1, blocking collectives, local(): full_rows = lax.all_gather(object_field, 'group', axis=1, tiled=True)  29.8 us
    dot_general x8, matrix products, apply_right(): jnp.einsum('pjk,kl->pjl', values, matrix, precision=lax.Precision.HIGHEST)  12.3 us
    dot_general x8, matrix products, apply_left(): jnp.einsum('jk,pkl->pjl', matrix, values, precision=lax.Precision.HIGHEST)  11.8 us
    dynamic_update_slice x1, local copies, waits for them, and re-layouts, place(): return lax.dynamic_update_slice(current, piece + terms[slot], corner)  10.9 us
    ppermute x2, starting transfers between devices, padded_2(): before = lax.ppermute(last, axis, up)  9.64 us
  transfers between devices with their start and end apart: 6, of which 2 were waited for; matrix products, arithmetic and copies ran while one was open for 2% of the time, Pallas kernels for 0%

commit v1 on v0

--- a/solution.py
+++ b/solution.py
@@ -129,7 +129,7 @@
     arrived = padded_2(edge_strips(accum), (("tile", 2),), HALO)
     summed = add_edges(accum[:, :, HALO : accum.shape[2] - HALO], arrived)
     share = lax.psum_scatter(summed, "group", scatter_dimension=1, tiled=True)
-    probe_grad, window_light = lax.psum((probe_grad, window_light), ("tile", "group"))
+    probe_grad, window_light = lax.psum(lax.psum((probe_grad, window_light), "group"), "tile")
     object_field, probe_field = apply_updates(
         object_field, probe_field, share, probe_grad, window_light
     )

time: 371 us -> 496 us (1.34)
  waiting for transfers between devices: 262 us -> 389 us
    psum x1 -> x2, waiting for transfers between devices: 258 us -> 342 us  [the longest x1 271 us: local(): lax.psum(lax.psum((probe_grad, window_light), 'group'), 'tile')]
    reduce_scatter x1, waiting for transfers between devices: 0.01 us -> 40.7 us  [local(): share = lax.psum_scatter(summed, 'group', scatter_dimension=1, tiled=True)]
  transfers between devices with their start and end apart: 6 -> 7, of which waited for: 2 -> 5; matrix products, arithmetic and copies ran while one was open for 2% -> 3% of each run, Pallas kernels for 0% -> 0%
where the time goes in v1:
time: 496 us; the launch traced here: 494 us
  waiting for transfers between devices  389 us (78%)
  blocking collectives  29.8 us (6%)
  matrix products  24.1 us (5%)
  between operations  17.3 us (3%)
  starting transfers between devices  12.3 us (2%)
  local copies, waits for them, and re-layouts  11.1 us (2%)
  other arithmetic  10.4 us (2%)
    psum x1, waiting for transfers between devices, local(): lax.psum(lax.psum((probe_grad, window_light), 'group'), 'tile')  271 us
    psum x1, waiting for transfers between devices, local(): lax.psum((probe_grad, window_light), 'group')  70.8 us
    reduce_scatter x1, waiting for transfers between devices, local(): share = lax.psum_scatter(summed, 'group', scatter_dimension=1, tiled=True)  40.7 us
    all_gather x1, blocking collectives, local(): full_rows = lax.all_gather(object_field, 'group', axis=1, tiled=True)  29.8 us
    dot_general x8, matrix products, apply_right(): jnp.einsum('pjk,kl->pjl', values, matrix, precision=lax.Precision.HIGHEST)  12.3 us
    dot_general x8, matrix products, apply_left(): jnp.einsum('jk,pkl->pjl', matrix, values, precision=lax.Precision.HIGHEST)  11.8 us
    dynamic_update_slice x1, local copies, waits for them, and re-layouts, place(): return lax.dynamic_update_slice(current, piece + terms[slot], corner)  10.9 us
  transfers between devices with their start and end apart: 7, of which 5 were waited for; matrix products, arithmetic and copies ran while one was open for 3% of the time, Pallas kernels for 0%

profile of v1, /device:TPU:2, one launch (start us, length us, event | category | flops | bytes accessed | tf_op | source)
XLA Modules:
  0.0 493.9 jit_solution(9146895240708930813)
XLA Ops:
  7.2 29.8 %all_gather.3 = f32[2,320,128]{2,1,0:T(8,128)S(1)} all-gather(f32[2,40,128]{2,1,0:T(8,128)} %param.14), channel_id=1, replica_groups=mesh['tile'=32,'group'=8] {'group'}, dimensions={1}, use_global_device_ids=true | all-gather | bytes 368640 | tf_op jit(solution)/shard_map/all_gather | solution.py:121
  38.3 3.1 collective-permute-start
  45.4 1.5 fusion.34
  46.8 1.5 fusion.9
  48.3 1.5 fusion.7
  49.8 1.5 fusion.47
  51.3 1.5 fusion.48
  52.8 1.5 fusion.4
  54.3 1.7 bitcast_multiply_fusion.11
  56.0 1.5 fusion.31
  59.0 1.5 fusion.3
  60.5 1.5 fusion.2
  62.0 1.5 fusion.45
  63.4 1.5 fusion.46
  64.9 1.5 fusion
  66.4 1.7 fusion.1
  70.7 10.9 %dynamic_update_slice.4 = f32[3,320,384]{2,1,0:T(8,128)S(1)} dynamic-update-slice(f32[3,320,384]{2,1,0:T(8,128)S(1)} %broadcast_in_dim.6, f32[3,256,256]{2,1,0:T(8,128)S(1)} %maximum_bitcast_fusion, s32[]{:T(128)} %constant.112.clone.1, s32[]{:T(128)S(6)} %select_n.60, s32[]{:T(128)S(6)} %select_n.61) | dynamic-update-slice | bytes 1572868 | tf_op jit(solution)/shard_map/while/body/eval_jaxpr/dynamic_update_slice | solution.py:86
  81.7 6.6 %collective-permute-start.2 = (f32[3,320,128]{2,1,0:T(8,128)S(1)}, f32[3,320,128]{2,1,0:T(8,128)S(1)}, u32[]{:S(2)}, u32[]{:S(2)}) collective-permute-start(f32[3,320,128]{2,1,0:T(8,128)S(1)} %get-tuple-element.75), channel_id=1, source_target_pairs={{0,8},{8,16},{16,24},{24,32},{32,40},{40,48},{48,56},{56,64},{64,7... | collective-permute-start | bytes 1474568 | tf_op jit(solution)/shard_map/ppermute | solution.py:18
  89.8 5.9 %collective-permute-done.3 = f32[3,320,128]{2,1,0:T(8,128)S(1)} collective-permute-done((f32[3,320,128]{2,1,0:T(8,128)S(1)}, f32[3,320,128]{2,1,0:T(8,128)S(1)}, u32[]{:S(2)}, u32[]{:S(2)}) %collective-permute-start.3) | collective-permute-done | bytes 491552 | tf_op jit(solution)/shard_map/ppermute | solution.py:19
  96.7 70.8 %all-reduce.7.cloned.1.call-done = (f32[2,256,256]{2,1,0:T(8,128)}, f32[256,256]{1,0:T(8,128)}) async-done(((f32[2,256,256]{2,1,0:T(8,128)}, f32[256,256]{1,0:T(8,128)}), (f32[2,256,256]{2,1,0:T(8,128)}, f32[256,256]{1,0:T(8,128)})) %all-reduce.7.cloned.1.call-update) | async-done | bytes 786448 | tf_op jit(solution)/shard_map/psum | solution.py:132
  168.1 40.7 %reduce-scatter.2.cloned.1.call-done = f32[3,40,128]{2,1,0:T(8,128)} async-done(((f32[3,320,128]{2,1,0:T(8,128)}), f32[3,40,128]{2,1,0:T(8,128)}) %reduce-scatter.2.cloned.1.call-update) | async-done | bytes 61456 | tf_op jit(solution)/shard_map/reduce_scatter | solution.py:131
  210.9 271.2 %all-reduce.5.cloned.1.call-done = (f32[2,256,256]{2,1,0:T(8,128)}, f32[256,256]{1,0:T(8,128)}) async-done(((f32[2,256,256]{2,1,0:T(8,128)}, f32[256,256]{1,0:T(8,128)}), (f32[2,256,256]{2,1,0:T(8,128)}, f32[256,256]{1,0:T(8,128)})) %all-reduce.5.cloned.1.call-update) | async-done | bytes 786448 | tf_op jit(solution)/shard_map/psum | solution.py:132
  482.1 1.6 reduce_sum.8
  485.4 1.9 divide_subtract_fusion
  (31 shorter events, 12.9 us)
Async XLA Ops:
  7.2 36.6 %copy-start = (f32[2,256,256]{2,1,0:T(8,128)S(1)}, f32[2,256,256]{2,1,0:T(8,128)}, u32[]{:S(2)}) copy-start(f32[2,256,256]{2,1,0:T(8,128)} %param.15) | copy-start | bytes 1572868
  7.2 160.3 %all-reduce.7.cloned.1.call-start = ((), (), s32[]{:S(2)}) async-start(), calls=%async_computation.3 | async-start | bytes 1572864 | tf_op jit(solution)/shard_map/psum | solution.py:132
  37.0 6.3 %collective-permute-start.1 = (f32[2,320,128]{2,1,0:T(8,128)S(1)}, f32[2,320,128]{2,1,0:T(8,128)S(1)}, u32[]{:S(2)}, u32[]{:S(2)}) collective-permute-start(f32[2,320,128]{2,1,0:T(8,128)S(1)} %all_gather.3), channel_id=1, source_target_pairs={{8,0},{16,8},{24,16},{32,24},{40,32},{48,40},{56,48},{64,56},{72,6... | collective-permute-start | bytes 983048 | tf_op jit(solution)/shard_map/ppermute | solution.py:19
  38.3 5.0 %collective-permute-start = (f32[2,320,128]{2,1,0:T(8,128)S(1)}, f32[2,320,128]{2,1,0:T(8,128)S(1)}, u32[]{:S(2)}, u32[]{:S(2)}) collective-permute-start(f32[2,320,128]{2,1,0:T(8,128)S(1)} %all_gather.3), channel_id=1, source_target_pairs={{0,8},{8,16},{16,24},{24,32},{32,40},{40,48},{48,56},{56,64},{64,7... | collective-permute-start | bytes 983048 | tf_op jit(solution)/shard_map/ppermute | solution.py:18
  51.3 3.0 copy-start.2
  70.5 138.3 %reduce-scatter.2.cloned.1.call-start = ((), (), s32[]{:S(2)}) async-start(), calls=%async_computation.1 | async-start | bytes 552960 | tf_op jit(solution)/shard_map/reduce_scatter | solution.py:131
  81.7 8.1 %collective-permute-start.2 = (f32[3,320,128]{2,1,0:T(8,128)S(1)}, f32[3,320,128]{2,1,0:T(8,128)S(1)}, u32[]{:S(2)}, u32[]{:S(2)}) collective-permute-start(f32[3,320,128]{2,1,0:T(8,128)S(1)} %get-tuple-element.75), channel_id=1, source_target_pairs={{0,8},{8,16},{16,24},{24,32},{32,40},{40,48},{48,56},{56,64},{64,7... | collective-permute-start | bytes 1474568 | tf_op jit(solution)/shard_map/ppermute | solution.py:18
  88.3 121.2 %copy-start.1 = (f32[2,40,128]{2,1,0:T(8,128)S(1)}, f32[2,40,128]{2,1,0:T(8,128)}, u32[]{:S(2)}) copy-start(f32[2,40,128]{2,1,0:T(8,128)} %param.14) | copy-start | bytes 122884
  88.3 7.4 %collective-permute-start.3 = (f32[3,320,128]{2,1,0:T(8,128)S(1)}, f32[3,320,128]{2,1,0:T(8,128)S(1)}, u32[]{:S(2)}, u32[]{:S(2)}) collective-permute-start(f32[3,320,128]{2,1,0:T(8,128)S(1)} %get-tuple-element.76), channel_id=1, source_target_pairs={{8,0},{16,8},{24,16},{32,24},{40,32},{48,40},{56,48},{64,56},{72,6... | collective-permute-start | bytes 1474568 | tf_op jit(solution)/shard_map/ppermute | solution.py:19
  96.6 385.5 %all-reduce.5.cloned.1.call-start = ((), (), s32[]{:S(2)}) async-start(), calls=%async_computation.2 | async-start | bytes 1572864 | tf_op jit(solution)/shard_map/psum | solution.py:132
Sparse Core Ops, SparseCore 0:
  70.6 96.7 all-reduce.6
  170.1 38.6 reduce-scatter.1
  211.5 270.6 all-reduce.4
